TPU v7x, 512 devices: a whole 4x4x16 slice. The times are simulated.
512 devices in a mesh: ctx: 32 (over x, z_lo, core), tp: 16 (over y, z_hi).
Axes of the slice: x: 4, y: 4, z: 16 (z_hi: 4, z_lo: 4; z = z_hi * 4 + z_lo), core: 2. Of those that a mesh axis runs over, the one named last changes fastest.
Arguments:
- attention_out: bfloat16 [512, 8192], P('ctx', 'tp'), may hold values from -6 to 6
- w_out: bfloat16 [8192, 8192], P('tp', 'ctx'), may hold values from -0.0625 to 0.0625
- residual: bfloat16 [512, 8192], P(('ctx', 'tp')), may hold values from -6 to 6
- norm_gain: float32 [8192], replicated, may hold values from 0.1 to 1.9
- w_gate: bfloat16 [28672, 8192], P(('ctx', 'tp')), may hold values from -0.0625 to 0.0625
- w_up: bfloat16 [28672, 8192], P(('ctx', 'tp')), may hold values from -0.0625 to 0.0625
- w_down: bfloat16 [32, 896, 8192], P(None, 'tp', 'ctx'), may hold values from -0.03125 to 0.03125
Outputs:
- mixed: bfloat16 [512, 8192], P(('ctx', 'tp'))
All inputs are finite; a program needn't handle non-finite values.
Results may differ from a plain program's by a relative error of at most 0.02.
Values may be sent and summed in bfloat16 or wider, within the bound.
No kernel may reach another device: no remote copies, remote signals or barrier semaphores. Data moves between devices by JAX's collectives and lax.ppermute only.
A program may use at most 64 MiB of HBM per device.

v0:
```python
import jax
import jax.numpy as jnp
from jax import lax
from jax.sharding import PartitionSpec as P


def owner_order(partial_value, ctx_count, tp_count, row_count):
    col_count = partial_value.shape[1]
    grouped = partial_value.reshape(ctx_count, tp_count, row_count, col_count)
    return jnp.transpose(grouped, (1, 0, 2, 3)).reshape(tp_count * ctx_count * row_count, col_count)


def shards(attention_out, w_out, residual, norm_gain, w_gate, w_up, w_down):
    row_count = residual.shape[0]
    ctx_count = lax.axis_size("ctx")
    tp_count = lax.axis_size("tp")
    unit_count = w_gate.shape[0]
    col_count = w_down.shape[2]
    partial_value = jnp.dot(
        lax.all_gather(attention_out, "ctx", axis=0, tiled=True),
        w_out,
        preferred_element_type=jnp.float32,
    )
    summed = lax.psum_scatter(
        owner_order(partial_value, ctx_count, tp_count, row_count).astype(jnp.bfloat16),
        "tp",
        scatter_dimension=0,
        tiled=True,
    ).astype(jnp.float32)
    proj = lax.all_to_all(
        summed.astype(jnp.bfloat16), "ctx", split_axis=0, concat_axis=1, tiled=True
    ).astype(summed.dtype)
    carried = residual.astype(jnp.float32) + proj
    mean_square = jnp.mean(carried * carried, axis=-1, keepdims=True)
    normed = (carried * lax.rsqrt(mean_square + 1e-05) * norm_gain).astype(jnp.bfloat16)
    paired = jnp.concatenate([w_gate, w_up], axis=0)
    group = lax.all_gather(normed, "tp", axis=0, tiled=True)
    gate_up = lax.dot_general(
        lax.all_gather(group, "ctx", axis=0, tiled=True),
        paired,
        (((1,), (1,)), ((), ())),
        preferred_element_type=jnp.float32,
    )
    gate_part = gate_up[:, :unit_count]
    up_part = gate_up[:, unit_count:]
    hidden = (jax.nn.silu(gate_part) * up_part).astype(jnp.bfloat16)
    flat_down = w_down.reshape(ctx_count * unit_count, col_count)
    partial_down = jnp.dot(
        lax.all_gather(hidden, "ctx", axis=1, tiled=True),
        flat_down,
        preferred_element_type=jnp.float32,
    )
    reduced = lax.psum_scatter(
        owner_order(partial_down, ctx_count, tp_count, row_count).astype(jnp.bfloat16),
        "tp",
        scatter_dimension=0,
        tiled=True,
    ).astype(jnp.float32)
    down = lax.all_to_all(
        reduced.astype(jnp.bfloat16), "ctx", split_axis=0, concat_axis=1, tiled=True
    ).astype(reduced.dtype)
    return (carried + down).astype(jnp.bfloat16)


def solution(mesh):
    in_specs = (
        P("ctx", "tp"),
        P("tp", "ctx"),
        P(("ctx", "tp"), None),
        P(),
        P(("ctx", "tp"), None),
        P(("ctx", "tp"), None),
        P(None, "tp", "ctx"),
    )
    out_specs = P(("ctx", "tp"), None)
    return jax.shard_map(shards, mesh=mesh, in_specs=in_specs, out_specs=out_specs, check_vma=False)
```

profile of v0, /device:TPU:1, one launch (start us, length us, event | category | flops | bytes accessed | tf_op | source)
XLA Modules:
  0.0 513.3 jit_solution(6987445112993718375)
XLA Ops:
  6.5 48.2 %all_gather.12 = bf16[512,512]{1,0:T(8,128)(2,1)S(1)} all-gather(bf16[16,512]{1,0:T(8,128)(2,1)} %param.7), channel_id=1, replica_groups=mesh['ctx'=32,'tp'=16] {'ctx'}, dimensions={0}, use_global_device_ids=true | all-gather | bytes 540672 | tf_op jit(solution)/shard_map/all_gather | solution.py:20
  54.7 1.4 convolution_convert_fusion.1
  56.1 0.8 copy.12
  56.9 0.0 all-gather.4.cloned.1.call-start
  56.9 108.8 %reduce-scatter.3.cloned.1.call-done = bf16[32,256]{1,0:T(8,128)(2,1)} async-done(((bf16[512,256]{1,0:T(8,128)(2,1)}), bf16[32,256]{1,0:T(8,128)(2,1)}) %reduce-scatter.3.cloned.1.call-update) | async-done | bytes 16400 | tf_op jit(solution)/shard_map/reduce_scatter | solution.py:24
  165.8 0.5 broadcast.4
  166.3 1.4 reduce.1
  167.6 14.4 %all_to_all.26 = bf16[32,2,128]{2,1,0:T(2,128)(2,1)S(1)} all-to-all(bf16[32,2,128]{2,1,0:T(2,128)(2,1)S(1)} %reshape.72), channel_id=1, replica_groups=mesh['ctx'=32,'tp'=16] {'ctx'}, dimensions={0} | all-to-all | bytes 32768 | tf_op jit(solution)/shard_map/all_to_all | solution.py:30
  182.1 0.7 multiply_reduce_fusion
  183.5 0.1 convert_bitcast_fusion
  183.6 50.3 %all-gather = bf16[16,1,8192]{2,1,0:T(2,128)(2,1)S(1)} all-gather(bf16[1,1,8192]{2,1,0:T(2,128)(2,1)S(1)} %convert_bitcast_fusion), channel_id=1, replica_groups=mesh['ctx'=32,'tp'=16] {'tp'}, dimensions={0}, use_global_device_ids=true | all-gather | bytes 278528 | tf_op jit(solution)/shard_map/all_gather | solution.py:37
  233.9 1.0 copy.19
  235.0 71.6 %all-gather.4.cloned.1.call-done = bf16[512,8192]{1,0:T(8,128)(2,1)} async-done(((bf16[16,8192]{1,0:T(8,128)(2,1)}), bf16[512,8192]{1,0:T(8,128)(2,1)}) %all-gather.4.cloned.1.call-update) | async-done | bytes 8388624 | tf_op jit(solution)/shard_map/all_gather | solution.py:39
  306.5 6.2 %fusion = f32[512,112]{0,1:T(8,128)S(1)} fusion(bf16[512,8192]{1,0:T(8,128)(2,1)} %all-gather.4.cloned.1.call-done, bf16[56,8192]{1,0:T(8,128)(2,1)S(1)} %copy-done.3, bf16[56,8192]{1,0:T(8,128)(2,1)S(1)} %copy-done.4), kind=kOutput, calls=%fused_computation | convolution fusion | flops 943194112 | bytes 10452992 | tf_op jit(solution)/shard_map/dot_general | solution.py:38
  312.8 0.7 fusion.5
  313.5 0.0 reduce-scatter.5.cloned.1.call-start
  313.5 64.0 %all-gather.6.cloned.1.call-done = bf16[512,1792]{0,1:T(8,128)(2,1)} async-done(((bf16[512,56]{0,1:T(8,128)(2,1)}), bf16[512,1792]{0,1:T(8,128)(2,1)}) %all-gather.6.cloned.1.call-update) | async-done | bytes 1835024 | tf_op jit(solution)/shard_map/all_gather | solution.py:49
  377.5 2.8 copy.14
  380.3 0.6 fusion.4
  380.9 0.8 copy.15
  381.7 108.5 %reduce-scatter.5.cloned.1.call-done = bf16[32,256]{1,0:T(8,128)(2,1)} async-done(((bf16[512,256]{1,0:T(8,128)(2,1)}), bf16[32,256]{1,0:T(8,128)(2,1)}) %reduce-scatter.5.cloned.1.call-update) | async-done | bytes 16400 | tf_op jit(solution)/shard_map/reduce_scatter | solution.py:53
  490.3 1.4 reduce.2
  491.6 14.4 %all_to_all.27 = bf16[32,2,128]{2,1,0:T(2,128)(2,1)S(1)} all-to-all(bf16[32,2,128]{2,1,0:T(2,128)(2,1)S(1)} %reshape.74), channel_id=1, replica_groups=mesh['ctx'=32,'tp'=16] {'ctx'}, dimensions={0} | all-to-all | bytes 32768 | tf_op jit(solution)/shard_map/all_to_all | solution.py:59
  506.1 0.7 fusion.6
  (20 shorter events, 0.2 us)
Async XLA Ops:
  6.5 373.7 %copy-start = (bf16[32,56,256]{2,1,0:T(8,128)(2,1)S(1)}, bf16[32,56,256]{2,1,0:T(8,128)(2,1)}, u32[]{:S(2)}) copy-start(bf16[32,56,256]{2,1,0:T(8,128)(2,1)} %param.13) | copy-start | bytes 2752516
  6.5 175.5 %copy-start.1 = (bf16[1,8192]{1,0:T(2,128)(2,1)S(1)}, bf16[1,8192]{1,0:T(2,128)(2,1)}, u32[]{:S(2)}) copy-start(bf16[1,8192]{1,0:T(2,128)(2,1)} %param.9) | copy-start | bytes 49156
  6.5 176.9 %copy-start.2 = (f32[8192]{0:T(1024)S(1)}, f32[8192]{0:T(1024)}, u32[]{:S(2)}) copy-start(f32[8192]{0:T(1024)} %param.10) | copy-start | bytes 98308
  6.5 159.2 %reduce-scatter.3.cloned.1.call-start = ((), (), s32[]{:S(2)}) async-start(), calls=%async_computation.4 | async-start | bytes 278528 | tf_op jit(solution)/shard_map/reduce_scatter | solution.py:24
  54.7 251.8 %copy-start.3 = (bf16[56,8192]{1,0:T(8,128)(2,1)S(1)}, bf16[56,8192]{1,0:T(8,128)(2,1)}, u32[]{:S(2)}) copy-start(bf16[56,8192]{1,0:T(8,128)(2,1)} %param.12) | copy-start | bytes 2752516
  54.7 251.8 %copy-start.4 = (bf16[56,8192]{1,0:T(8,128)(2,1)S(1)}, bf16[56,8192]{1,0:T(8,128)(2,1)}, u32[]{:S(2)}) copy-start(bf16[56,8192]{1,0:T(8,128)(2,1)} %param.11) | copy-start | bytes 2752516
  56.9 249.6 %all-gather.4.cloned.1.call-start = ((), (), s32[]{:S(2)}) async-start(), calls=%async_computation.5 | async-start | bytes 8650752 | tf_op jit(solution)/shard_map/all_gather | solution.py:39
  234.9 142.6 %all-gather.6.cloned.1.call-start = ((), (), s32[]{:S(2)}) async-start(), calls=%async_computation.6 | async-start | bytes 1892352 | tf_op jit(solution)/shard_map/all_gather | solution.py:49
  313.5 176.8 %reduce-scatter.5.cloned.1.call-start = ((), (), s32[]{:S(2)}) async-start(), calls=%async_computation.7 | async-start | bytes 278528 | tf_op jit(solution)/shard_map/reduce_scatter | solution.py:53
Sparse Core Ops, SparseCore 0:
  57.0 108.6 reduce-scatter.2
  235.0 71.4 all-gather.3
  313.6 63.8 all-gather.5
  381.9 108.2 reduce-scatter.4
where the time goes:
time: 514 us; the launch traced here: 513 us
  waiting for transfers between devices  353 us (69%)
  blocking collectives  127 us (25%)
  between operations  13.9 us (3%)
  matrix products  8.23 us (2%)
  local copies, waits for them, and re-layouts  5.9 us (1%)
    reduce_scatter x1, waiting for transfers between devices, shards(): lax.psum_scatter(owner_order(partial_value, ctx_count, tp_count, row_coun...  109 us
    reduce_scatter x1, waiting for transfers between devices, shards(): lax.psum_scatter(owner_order(partial_down, ctx_count, tp_count, row_count...  109 us
    all_gather x1, waiting for transfers between devices, shards(): lax.all_gather(group, 'ctx', axis=0, tiled=True)  71.6 us
    all_gather x1, waiting for transfers between devices, shards(): lax.all_gather(hidden, 'ctx', axis=1, tiled=True)  64 us
    all_gather x1, blocking collectives, shards(): group = lax.all_gather(normed, 'tp', axis=0, tiled=True)  50.3 us
    all_gather x1, blocking collectives, shards(): lax.all_gather(attention_out, 'ctx', axis=0, tiled=True)  48.2 us
    all_to_all x1, blocking collectives, shards(): lax.all_to_all(reduced.astype(jnp.bfloat16), 'ctx', split_axis=0, concat_...  14.4 us
    all_to_all x1, blocking collectives, shards(): lax.all_to_all(summed.astype(jnp.bfloat16), 'ctx', split_axis=0, concat_a...  14.4 us
  transfers between devices with their start and end apart: 4, of which 4 were waited for; matrix products, arithmetic and copies ran while one was open for 0% of the time, Pallas kernels for 0%

commit v1 on v0

--- a/solution.py
+++ b/solution.py
@@ -2,6 +2,13 @@
 import jax.numpy as jnp
 from jax import lax
 from jax.sharding import PartitionSpec as P
+
+
+def replace_lane(vals):
+    extra = jnp.concatenate(
+        lax.all_to_all(jnp.stack(jnp.split(vals, lax.axis_size("ctx"), 0), 0), "ctx", 0, 0), 1
+    )
+    return extra
 
 
 def owner_order(partial_value, ctx_count, tp_count, row_count):
@@ -56,9 +63,7 @@
         scatter_dimension=0,
         tiled=True,
     ).astype(jnp.float32)
-    down = lax.all_to_all(
-        reduced.astype(jnp.bfloat16), "ctx", split_axis=0, concat_axis=1, tiled=True
-    ).astype(reduced.dtype)
+    down = replace_lane(reduced.astype(jnp.bfloat16)).astype(reduced.dtype)
     return (carried + down).astype(jnp.bfloat16)
 
 

time: 514 us -> 536 us (1.043)
  local copies, waits for them, and re-layouts: 5.9 us -> 27.9 us
    unnamed x15 -> x46, local copies, waits for them, and re-layouts: 1.09 us -> 22.4 us
where the time goes in v1:
time: 536 us; the launch traced here: 535 us
  waiting for transfers between devices  353 us (66%)
  blocking collectives  127 us (24%)
  local copies, waits for them, and re-layouts  27.9 us (5%)
  between operations  13.9 us (3%)
  matrix products  8.23 us (2%)
    reduce_scatter x1, waiting for transfers between devices, shards(): lax.psum_scatter(owner_order(partial_value, ctx_count, tp_count, row_coun...  109 us
    reduce_scatter x1, waiting for transfers between devices, shards(): lax.psum_scatter(owner_order(partial_down, ctx_count, tp_count, row_count...  109 us
    all_gather x1, waiting for transfers between devices, shards(): lax.all_gather(group, 'ctx', axis=0, tiled=True)  71.6 us
    all_gather x1, waiting for transfers between devices, shards(): lax.all_gather(hidden, 'ctx', axis=1, tiled=True)  64 us
    all_gather x1, blocking collectives, shards(): group = lax.all_gather(normed, 'tp', axis=0, tiled=True)  50.3 us
    all_gather x1, blocking collectives, shards(): lax.all_gather(attention_out, 'ctx', axis=0, tiled=True)  48.2 us
    unnamed x46, local copies, waits for them, and re-layouts  22.4 us
    all_to_all x1, blocking collectives, replace_lane(): lax.all_to_all(jnp.stack(jnp.split(vals, lax.axis_size('ctx'), 0), 0), 'c...  14.4 us
  transfers between devices with their start and end apart: 4, of which 4 were waited for; matrix products, arithmetic and copies ran while one was open for 0% of the time, Pallas kernels for 0%

profile of v1, /device:TPU:1, one launch (start us, length us, event | category | flops | bytes accessed | tf_op | source)
XLA Modules:
  0.0 534.7 jit_solution(765502621927711339)
XLA Ops:
  6.5 48.2 %all_gather.12 = bf16[512,512]{1,0:T(8,128)(2,1)S(1)} all-gather(bf16[16,512]{1,0:T(8,128)(2,1)} %param.7), channel_id=1, replica_groups=mesh['ctx'=32,'tp'=16] {'ctx'}, dimensions={0}, use_global_device_ids=true | all-gather | bytes 540672 | tf_op jit(solution)/shard_map/all_gather | solution.py:27
  54.7 1.4 convolution_convert_fusion.1
  56.1 0.8 copy.12
  56.9 108.8 %reduce-scatter.3.cloned.1.call-done = bf16[32,256]{1,0:T(8,128)(2,1)} async-done(((bf16[512,256]{1,0:T(8,128)(2,1)}), bf16[32,256]{1,0:T(8,128)(2,1)}) %reduce-scatter.3.cloned.1.call-update) | async-done | bytes 16400 | tf_op jit(solution)/shard_map/reduce_scatter | solution.py:31
  166.3 1.4 reduce.1
  167.6 14.4 %all_to_all.18 = bf16[32,2,128]{2,1,0:T(2,128)(2,1)S(1)} all-to-all(bf16[32,2,128]{2,1,0:T(2,128)(2,1)S(1)} %reshape.67), channel_id=1, replica_groups=mesh['ctx'=32,'tp'=16] {'ctx'}, dimensions={0} | all-to-all | bytes 32768 | tf_op jit(solution)/shard_map/all_to_all | solution.py:37
  182.1 0.7 multiply_reduce_fusion
  183.6 50.3 %all-gather = bf16[16,1,8192]{2,1,0:T(2,128)(2,1)S(1)} all-gather(bf16[1,1,8192]{2,1,0:T(2,128)(2,1)S(1)} %convert_bitcast_fusion), channel_id=1, replica_groups=mesh['ctx'=32,'tp'=16] {'tp'}, dimensions={0}, use_global_device_ids=true | all-gather | bytes 278528 | tf_op jit(solution)/shard_map/all_gather | solution.py:44
  233.9 1.0 copy.18
  235.0 71.6 %all-gather.4.cloned.1.call-done = bf16[512,8192]{1,0:T(8,128)(2,1)} async-done(((bf16[16,8192]{1,0:T(8,128)(2,1)}), bf16[512,8192]{1,0:T(8,128)(2,1)}) %all-gather.4.cloned.1.call-update) | async-done | bytes 8388624 | tf_op jit(solution)/shard_map/all_gather | solution.py:46
  306.5 6.2 %fusion = f32[512,112]{0,1:T(8,128)S(1)} fusion(bf16[512,8192]{1,0:T(8,128)(2,1)} %all-gather.4.cloned.1.call-done, bf16[56,8192]{1,0:T(8,128)(2,1)S(1)} %copy-done.3, bf16[56,8192]{1,0:T(8,128)(2,1)S(1)} %copy-done.4), kind=kOutput, calls=%fused_computation | convolution fusion | flops 943194112 | bytes 10452992 | tf_op jit(solution)/shard_map/dot_general | solution.py:45
  313.5 64.0 %all-gather.6.cloned.1.call-done = bf16[512,1792]{0,1:T(8,128)(2,1)} async-done(((bf16[512,56]{0,1:T(8,128)(2,1)}), bf16[512,1792]{0,1:T(8,128)(2,1)}) %all-gather.6.cloned.1.call-update) | async-done | bytes 1835024 | tf_op jit(solution)/shard_map/all_gather | solution.py:56
  377.5 2.8 copy.14
  380.9 0.8 copy.15
  381.7 108.5 %reduce-scatter.5.cloned.1.call-done = bf16[32,256]{1,0:T(8,128)(2,1)} async-done(((bf16[512,256]{1,0:T(8,128)(2,1)}), bf16[32,256]{1,0:T(8,128)(2,1)}) %reduce-scatter.5.cloned.1.call-update) | async-done | bytes 16400 | tf_op jit(solution)/shard_map/reduce_scatter | solution.py:60
  507.4 0.7 constant_dynamic-update-slice_fusion.6
  508.1 0.7 constant_dynamic-update-slice_fusion.5
  508.8 0.7 constant_dynamic-update-slice_fusion.4
  509.5 0.7 constant_dynamic-update-slice_fusion.3
  510.2 0.7 constant_dynamic-update-slice_fusion.2
  510.9 0.7 constant_dynamic-update-slice_fusion.1
  511.6 0.7 constant_dynamic-update-slice_fusion
  512.3 0.7 reduce.2
  513.1 14.4 %all_to_all.19 = bf16[32,2,128]{2,1,0:T(2,128)(2,1)S(1)} all-to-all(bf16[32,2,128]{2,1,0:T(2,128)(2,1)S(1)} %reshape.69), channel_id=1, replica_groups=mesh['ctx'=32,'tp'=16] {'ctx'}, dimensions={0} | all-to-all | bytes 32768 | tf_op jit(solution)/shard_map/all_to_all | solution.py:9
  (52 shorter events, 20.0 us)
Async XLA Ops:
  6.5 373.7 %copy-start = (bf16[32,56,256]{2,1,0:T(8,128)(2,1)S(1)}, bf16[32,56,256]{2,1,0:T(8,128)(2,1)}, u32[]{:S(2)}) copy-start(bf16[32,56,256]{2,1,0:T(8,128)(2,1)} %param.13) | copy-start | bytes 2752516
  6.5 175.5 %copy-start.1 = (bf16[1,8192]{1,0:T(2,128)(2,1)S(1)}, bf16[1,8192]{1,0:T(2,128)(2,1)}, u32[]{:S(2)}) copy-start(bf16[1,8192]{1,0:T(2,128)(2,1)} %param.9) | copy-start | bytes 49156
  6.5 176.9 %copy-start.2 = (f32[8192]{0:T(1024)S(1)}, f32[8192]{0:T(1024)}, u32[]{:S(2)}) copy-start(f32[8192]{0:T(1024)} %param.10) | copy-start | bytes 98308
  6.5 159.2 %reduce-scatter.3.cloned.1.call-start = ((), (), s32[]{:S(2)}) async-start(), calls=%async_computation.4 | async-start | bytes 278528 | tf_op jit(solution)/shard_map/reduce_scatter | solution.py:31
  54.7 251.8 %copy-start.3 = (bf16[56,8192]{1,0:T(8,128)(2,1)S(1)}, bf16[56,8192]{1,0:T(8,128)(2,1)}, u32[]{:S(2)}) copy-start(bf16[56,8192]{1,0:T(8,128)(2,1)} %param.12) | copy-start | bytes 2752516
  54.7 251.8 %copy-start.4 = (bf16[56,8192]{1,0:T(8,128)(2,1)S(1)}, bf16[56,8192]{1,0:T(8,128)(2,1)}, u32[]{:S(2)}) copy-start(bf16[56,8192]{1,0:T(8,128)(2,1)} %param.11) | copy-start | bytes 2752516
  56.9 249.6 %all-gather.4.cloned.1.call-start = ((), (), s32[]{:S(2)}) async-start(), calls=%async_computation.5 | async-start | bytes 8650752 | tf_op jit(solution)/shard_map/all_gather | solution.py:46
  234.9 142.6 %all-gather.6.cloned.1.call-start = ((), (), s32[]{:S(2)}) async-start(), calls=%async_computation.6 | async-start | bytes 1892352 | tf_op jit(solution)/shard_map/all_gather | solution.py:56
  313.5 176.8 %reduce-scatter.5.cloned.1.call-start = ((), (), s32[]{:S(2)}) async-start(), calls=%async_computation.7 | async-start | bytes 278528 | tf_op jit(solution)/shard_map/reduce_scatter | solution.py:60
Sparse Core Ops, SparseCore 0:
  57.0 108.6 reduce-scatter.2
  235.0 71.4 all-gather.3
  313.6 63.8 all-gather.5
  381.9 108.2 reduce-scatter.4
